TPU v7x, 256 devices: a whole 4x4x8 slice. The times are simulated.
256 devices in a mesh: ga: 4 (over z_hi), orb: 64 (over x, z_lo, y, core).
Axes of the slice: x: 4, y: 4, z: 8 (z_hi: 4, z_lo: 2; z = z_hi * 2 + z_lo), core: 2. Of those that a mesh axis runs over, the one named last changes fastest.
Arguments:
- coefficients: bfloat16 [2, 294912, 512], P(None, ('ga', 'orb')), may hold values from -0.01171875 to 0.01171875
- triples: int32 [3, 294912], P(None, ('ga', 'orb')), may hold values from -33 to 33
- elec_pos: float32 [3, 256], P(None, ('ga', 'orb')), may hold values from 0 to 1
- ion_pos: float32 [3, 128], replicated, may hold values from 0 to 1
- assignment: int32 [256], P(('ga', 'orb')), may hold values from 0 to 127
- rotation: int32 [256], P(('ga', 'orb')), may hold values from 0 to 63
- quad_table: float32 [64, 3, 12], replicated, may hold values from -2.4 to 2.4
- inverse_rows: float32 [256, 512], P(('ga', 'orb')), may hold values from -0.25 to 0.25
Outputs:
- ratios: float32 [256, 12], P(('ga', 'orb'))
All inputs are finite; a program needn't handle non-finite values.
Results may differ from a plain program's by a relative error of at most 0.0024.
Values may be sent and summed in bfloat16 or wider, within the bound.
No kernel may reach another device: no remote copies, remote signals or barrier semaphores. Data moves between devices by JAX's collectives and lax.ppermute only.
A program may use at most 64 MiB of HBM per device.

v0:
```python
import math
import jax
import jax.numpy as jnp
from jax import lax
from jax.sharding import PartitionSpec as P

TWO_PI = 2.0 * math.pi


def point_coords(elec_pos, ion_pos, assignment, rotation, quad_table):
    ion_rows = jnp.take(ion_pos, assignment, axis=1)
    offsets = elec_pos - ion_rows
    radius = jnp.sqrt(jnp.sum(offsets * offsets, axis=0))
    displace = jnp.take(quad_table, rotation, axis=0)
    located = ion_rows.T[:, :, None] + radius[:, None, None] * displace
    return jnp.transpose(located, (1, 0, 2)).reshape(3, -1)


def phase_values(points, triples, coefficients):
    point_count = points.shape[1]
    wave_count = triples.shape[1]
    columns = coefficients.shape[2]
    block_rows = math.gcd(point_count, 512)
    waves = triples.astype(jnp.float32) * TWO_PI

    def one_block(block_points):

        def add_panel(step_index, running):
            angle = (
                block_points[0][:, None] * waves[0][None, :]
                + block_points[1][:, None] * waves[1][None, :]
                + block_points[2][:, None] * waves[2][None, :]
            )
            phases = jnp.concatenate(
                [jnp.cos(angle).astype(jnp.bfloat16), jnp.sin(angle).astype(jnp.bfloat16)], axis=1
            )
            weights = coefficients.reshape(2 * wave_count, columns)
            return running + jnp.dot(phases, weights, preferred_element_type=jnp.float32)

        initial = jnp.zeros((block_rows, columns), jnp.float32)
        return lax.fori_loop(0, wave_count // wave_count, add_panel, initial)

    blocks = jnp.transpose(points.reshape(3, point_count // block_rows, block_rows), (1, 0, 2))
    return lax.map(one_block, blocks).reshape(point_count, columns)


def on_device(
    coefficients, triples, elec_pos, ion_pos, assignment, rotation, quad_table, inverse_rows
):
    local_points = point_coords(elec_pos, ion_pos, assignment, rotation, quad_table)
    all_points = lax.all_gather(local_points, ("ga", "orb"), axis=1, tiled=True)
    electrons = inverse_rows.shape[0]
    values = lax.psum_scatter(
        phase_values(all_points, triples, coefficients),
        ("ga", "orb"),
        scatter_dimension=0,
        tiled=True,
    )
    shaped = values.reshape(electrons, values.shape[0] // electrons, values.shape[1])
    return jnp.sum(shaped * inverse_rows[:, None, :], axis=2)


def solution(mesh):
    return jax.shard_map(
        on_device,
        mesh=mesh,
        in_specs=(
            P(None, ("ga", "orb"), None),
            P(None, ("ga", "orb")),
            P(None, ("ga", "orb")),
            P(),
            P(("ga", "orb")),
            P(("ga", "orb")),
            P(),
            P(("ga", "orb"), None),
        ),
        out_specs=P(("ga", "orb"), None),
        check_vma=False,
    )
```

profile of v0, /device:TPU:192, one launch (start us, length us, event | category | flops | bytes accessed | tf_op | source)
XLA Modules:
  0.0 1629.5 jit_solution(16454387211662428138)
XLA Ops:
  5.1 307.0 %all-gather = f32[256,12,3]{1,2,0:T(4,128)S(1)} all-gather(f32[1,12,3]{1,2,0:T(4,128)S(1)} %add_bitcast_fusion), channel_id=1, replica_groups=mesh['ga'=4,'orb'=64] {'ga','orb'}, dimensions={0}, use_global_device_ids=true | all-gather | bytes 37008 | tf_op jit(solution)/shard_map/all_gather | solution.py:51
  313.2 70.7 %while.16 = (s32[]{:T(128)}, f32[6,512,512]{2,1,0:T(8,128)}, f32[6,3,512]{2,0,1:T(8,128)S(1)}, f32[3,1152]{1,0:T(4,128)S(1)}, bf16[2,1152,512]{2,1,0:T(8,128)(2,1)}, /*index=5*/s32[]{:T(128)}, s32[]{:T(128)}, s32[]{}, s32[]{}) while((s32[]{:T(128)}, f32[6,512,512]{2,1,0:T(8,128)}, f32[6,3,512]{2,0,1:T(8,128)S(1)}, f32[3,1152]{1,0:T(4,128)S(1)}, ...), condition=%wide.region_2.3_spmd, body=%wide.region_1.2_spmd.sunk | while | flops 1216806912 | bytes 17624220 | solution.py:44
  313.3 9.3 cosine_convert_fusion.2
  322.6 2.4 fusion.22
  325.1 9.3 cosine_convert_fusion.2
  334.4 2.4 fusion.22
  336.9 9.3 cosine_convert_fusion.2
  346.2 2.4 fusion.22
  348.6 9.3 cosine_convert_fusion.2
  357.9 2.4 fusion.22
  360.4 9.3 cosine_convert_fusion.2
  369.7 2.4 fusion.22
  372.2 9.3 cosine_convert_fusion.2
  381.5 2.4 fusion.22
  383.9 646.7 %fusion = f32[16,512]{1,0:T(8,128)S(1)} fusion(f32[3072,512]{1,0:T(8,128)} %bitcast.42), kind=kCustom, calls=%all-reduce-scatter | all-reduce-scatter fusion | flops 2097153 | bytes 6324224
  1030.6 85.6 %collective-permute-start = (f32[16,512]{1,0:T(8,128)S(1)}, f32[16,512]{1,0:T(8,128)S(1)}, u32[]{:S(2)}, u32[]{:S(2)}) collective-permute-start(f32[16,512]{1,0:T(8,128)S(1)} %fusion), channel_id=1, source_target_pairs={{0,1},{1,2},{2,3},{3,4},{4,5},{5,6},{6,7},{7,8},{8,9},{9,10},{10,1... | collective-permute-start | bytes 98312
  1116.2 13.1 collective-permute-start.1
  1129.3 13.1 collective-permute-start.10
  1143.8 14.8 collective-permute-start.11
  1158.6 13.1 collective-permute-start.12
  1171.8 13.1 collective-permute-start.13
  1184.9 13.1 collective-permute-start.14
  1198.0 13.1 collective-permute-start.15
  1211.2 13.1 collective-permute-start.16
  1224.3 13.1 collective-permute-start.17
  1237.5 13.1 collective-permute-start.18
  1250.6 13.1 collective-permute-start.19
  1263.7 13.1 collective-permute-start.2
  1276.9 13.1 collective-permute-start.20
  1290.0 13.1 collective-permute-start.21
  1303.2 13.1 collective-permute-start.22
  1316.3 13.1 collective-permute-start.23
  1329.4 13.1 collective-permute-start.24
  1342.6 13.1 collective-permute-start.25
  1355.7 13.1 collective-permute-start.26
  1368.9 13.1 collective-permute-start.27
  1382.0 13.1 collective-permute-start.28
  1395.1 6.0 collective-permute-start.29
  1401.1 10.8 collective-permute-start.3
  1411.9 5.7 collective-permute-start.30
  1417.6 3.9 collective-permute-start.31
  1425.5 1.9 collective-permute-start.34
  1431.3 1.9 collective-permute-start.37
  1435.2 1.9 collective-permute-start.39
  1437.1 24.4 %collective-permute-start.4 = (f32[16,512]{1,0:T(8,128)S(1)}, f32[16,512]{1,0:T(8,128)S(1)}, u32[]{:S(2)}, u32[]{:S(2)}) collective-permute-start(f32[16,512]{1,0:T(8,128)S(1)} %fusion), channel_id=1, source_target_pairs={{0,5},{1,6},{2,7},{3,8},{4,9},{5,10},{6,11},{7,12},{8,13},{9,14},{... | collective-permute-start | bytes 98312
  1461.6 4.9 collective-permute-start.40
  1466.5 2.5 collective-permute-start.41
  1469.0 1.9 collective-permute-start.42
  1471.0 2.2 collective-permute-start.43
  1475.2 2.4 collective-permute-start.45
  1479.5 1.9 collective-permute-start.47
  1485.3 20.8 %collective-permute-start.5 = (f32[16,512]{1,0:T(8,128)S(1)}, f32[16,512]{1,0:T(8,128)S(1)}, u32[]{:S(2)}, u32[]{:S(2)}) collective-permute-start(f32[16,512]{1,0:T(8,128)S(1)} %fusion), channel_id=1, source_target_pairs={{0,6},{1,7},{2,8},{3,9},{4,10},{5,11},{6,12},{7,13},{8,14},{9,15},... | collective-permute-start | bytes 98312
  1506.2 5.3 collective-permute-start.50
  1511.6 3.1 collective-permute-start.51
  1518.6 1.9 collective-permute-start.54
  1528.4 1.9 collective-permute-start.59
  1530.3 17.3 %collective-permute-start.6 = (f32[16,512]{1,0:T(8,128)S(1)}, f32[16,512]{1,0:T(8,128)S(1)}, u32[]{:S(2)}, u32[]{:S(2)}) collective-permute-start(f32[16,512]{1,0:T(8,128)S(1)} %fusion), channel_id=1, source_target_pairs={{0,7},{1,8},{2,9},{3,10},{4,11},{5,12},{6,13},{7,14},{8,15},{9,16}... | collective-permute-start | bytes 98312
  1547.6 6.5 collective-permute-start.60
  1554.1 1.9 collective-permute-start.61
  1558.0 12.6 collective-permute-start.7
  1570.7 13.1 collective-permute-start.8
  1583.9 13.3 collective-permute-start.9
  1598.6 7.0 collective-permute-done.9
  1605.6 23.3 %concatenate.6 = f32[1036,512]{1,0:T(8,128)S(1)} concatenate(f32[12,512]{1,0:T(8,128)S(1)} %collective-permute-done.63, f32[16,512]{1,0:T(8,128)} %copy-done.18, f32[16,512]{1,0:T(8,128)} %copy-done.17, f32[16,512]{1,0:T(8,128)} %copy-done.16, f32[16,512]{1,0:T(8,128)} %copy-done.14, f32[16,512]{1,0:T(8,128)} %copy-done.13, f32[16,512]{1,0:T(8,128)} %copy-done.12, ...), dimensions={0} | concatenate | bytes 4243456
  (159 shorter events, 38.6 us)
Async XLA Ops:
  1030.6 141.2 %collective-permute-start = (f32[16,512]{1,0:T(8,128)S(1)}, f32[16,512]{1,0:T(8,128)S(1)}, u32[]{:S(2)}, u32[]{:S(2)}) collective-permute-start(f32[16,512]{1,0:T(8,128)S(1)} %fusion), channel_id=1, source_target_pairs={{0,1},{1,2},{2,3},{3,4},{4,5},{5,6},{6,7},{7,8},{8,9},{9,10},{10,1... | collective-permute-start | bytes 98312
  1116.2 68.7 %collective-permute-start.1 = (f32[16,512]{1,0:T(8,128)S(1)}, f32[16,512]{1,0:T(8,128)S(1)}, u32[]{:S(2)}, u32[]{:S(2)}) collective-permute-start(f32[16,512]{1,0:T(8,128)S(1)} %fusion), channel_id=1, source_target_pairs={{0,2},{1,3},{2,4},{3,5},{4,6},{5,7},{6,8},{7,9},{8,10},{9,11},{10,... | collective-permute-start | bytes 98312
  1129.3 68.7 %collective-permute-start.10 = (f32[16,512]{1,0:T(8,128)S(1)}, f32[16,512]{1,0:T(8,128)S(1)}, u32[]{:S(2)}, u32[]{:S(2)}) collective-permute-start(f32[16,512]{1,0:T(8,128)S(1)} %fusion), channel_id=1, source_target_pairs={{0,11},{1,12},{2,13},{3,14},{4,15},{5,16},{6,17},{7,18},{8,19},{9,... | collective-permute-start | bytes 98312
  1142.5 16.2 collective-permute-start.63
  1143.8 67.4 %collective-permute-start.11 = (f32[16,512]{1,0:T(8,128)S(1)}, f32[16,512]{1,0:T(8,128)S(1)}, u32[]{:S(2)}, u32[]{:S(2)}) collective-permute-start(f32[16,512]{1,0:T(8,128)S(1)} %fusion), channel_id=1, source_target_pairs={{0,12},{1,13},{2,14},{3,15},{4,16},{5,17},{6,18},{7,19},{8,20},{9,... | collective-permute-start | bytes 98312
  1158.6 65.7 %collective-permute-start.12 = (f32[16,512]{1,0:T(8,128)S(1)}, f32[16,512]{1,0:T(8,128)S(1)}, u32[]{:S(2)}, u32[]{:S(2)}) collective-permute-start(f32[16,512]{1,0:T(8,128)S(1)} %fusion), channel_id=1, source_target_pairs={{0,13},{1,14},{2,15},{3,16},{4,17},{5,18},{6,19},{7,20},{8,21},{9,... | collective-permute-start | bytes 98312
  1171.8 65.7 %collective-permute-start.13 = (f32[16,512]{1,0:T(8,128)S(1)}, f32[16,512]{1,0:T(8,128)S(1)}, u32[]{:S(2)}, u32[]{:S(2)}) collective-permute-start(f32[16,512]{1,0:T(8,128)S(1)} %fusion), channel_id=1, source_target_pairs={{0,14},{1,15},{2,16},{3,17},{4,18},{5,19},{6,20},{7,21},{8,22},{9,... | collective-permute-start | bytes 98312
  1184.9 65.7 %collective-permute-start.14 = (f32[16,512]{1,0:T(8,128)S(1)}, f32[16,512]{1,0:T(8,128)S(1)}, u32[]{:S(2)}, u32[]{:S(2)}) collective-permute-start(f32[16,512]{1,0:T(8,128)S(1)} %fusion), channel_id=1, source_target_pairs={{0,15},{1,16},{2,17},{3,18},{4,19},{5,20},{6,21},{7,22},{8,23},{9,... | collective-permute-start | bytes 98312
  1198.0 65.7 %collective-permute-start.15 = (f32[16,512]{1,0:T(8,128)S(1)}, f32[16,512]{1,0:T(8,128)S(1)}, u32[]{:S(2)}, u32[]{:S(2)}) collective-permute-start(f32[16,512]{1,0:T(8,128)S(1)} %fusion), channel_id=1, source_target_pairs={{0,16},{1,17},{2,18},{3,19},{4,20},{5,21},{6,22},{7,23},{8,24},{9,... | collective-permute-start | bytes 98312
  1211.2 65.7 %collective-permute-start.16 = (f32[16,512]{1,0:T(8,128)S(1)}, f32[16,512]{1,0:T(8,128)S(1)}, u32[]{:S(2)}, u32[]{:S(2)}) collective-permute-start(f32[16,512]{1,0:T(8,128)S(1)} %fusion), channel_id=1, source_target_pairs={{0,17},{1,18},{2,19},{3,20},{4,21},{5,22},{6,23},{7,24},{8,25},{9,... | collective-permute-start | bytes 98312
  1224.3 65.7 %collective-permute-start.17 = (f32[16,512]{1,0:T(8,128)S(1)}, f32[16,512]{1,0:T(8,128)S(1)}, u32[]{:S(2)}, u32[]{:S(2)}) collective-permute-start(f32[16,512]{1,0:T(8,128)S(1)} %fusion), channel_id=1, source_target_pairs={{0,18},{1,19},{2,20},{3,21},{4,22},{5,23},{6,24},{7,25},{8,26},{9,... | collective-permute-start | bytes 98312
  1237.5 65.7 %collective-permute-start.18 = (f32[16,512]{1,0:T(8,128)S(1)}, f32[16,512]{1,0:T(8,128)S(1)}, u32[]{:S(2)}, u32[]{:S(2)}) collective-permute-start(f32[16,512]{1,0:T(8,128)S(1)} %fusion), channel_id=1, source_target_pairs={{0,19},{1,20},{2,21},{3,22},{4,23},{5,24},{6,25},{7,26},{8,27},{9,... | collective-permute-start | bytes 98312
  1250.6 65.7 %collective-permute-start.19 = (f32[16,512]{1,0:T(8,128)S(1)}, f32[16,512]{1,0:T(8,128)S(1)}, u32[]{:S(2)}, u32[]{:S(2)}) collective-permute-start(f32[16,512]{1,0:T(8,128)S(1)} %fusion), channel_id=1, source_target_pairs={{0,20},{1,21},{2,22},{3,23},{4,24},{5,25},{6,26},{7,27},{8,28},{9,... | collective-permute-start | bytes 98312
  1263.7 65.7 %collective-permute-start.2 = (f32[16,512]{1,0:T(8,128)S(1)}, f32[16,512]{1,0:T(8,128)S(1)}, u32[]{:S(2)}, u32[]{:S(2)}) collective-permute-start(f32[16,512]{1,0:T(8,128)S(1)} %fusion), channel_id=1, source_target_pairs={{0,3},{1,4},{2,5},{3,6},{4,7},{5,8},{6,9},{7,10},{8,11},{9,12},{10... | collective-permute-start | bytes 98312
  1276.9 65.7 %collective-permute-start.20 = (f32[16,512]{1,0:T(8,128)S(1)}, f32[16,512]{1,0:T(8,128)S(1)}, u32[]{:S(2)}, u32[]{:S(2)}) collective-permute-start(f32[16,512]{1,0:T(8,128)S(1)} %fusion), channel_id=1, source_target_pairs={{0,21},{1,22},{2,23},{3,24},{4,25},{5,26},{6,27},{7,28},{8,29},{9,... | collective-permute-start | bytes 98312
  1290.0 65.7 %collective-permute-start.21 = (f32[16,512]{1,0:T(8,128)S(1)}, f32[16,512]{1,0:T(8,128)S(1)}, u32[]{:S(2)}, u32[]{:S(2)}) collective-permute-start(f32[16,512]{1,0:T(8,128)S(1)} %fusion), channel_id=1, source_target_pairs={{0,22},{1,23},{2,24},{3,25},{4,26},{5,27},{6,28},{7,29},{8,30},{9,... | collective-permute-start | bytes 98312
  1303.2 65.7 %collective-permute-start.22 = (f32[16,512]{1,0:T(8,128)S(1)}, f32[16,512]{1,0:T(8,128)S(1)}, u32[]{:S(2)}, u32[]{:S(2)}) collective-permute-start(f32[16,512]{1,0:T(8,128)S(1)} %fusion), channel_id=1, source_target_pairs={{0,23},{1,24},{2,25},{3,26},{4,27},{5,28},{6,29},{7,30},{8,31},{9,... | collective-permute-start | bytes 98312
  1316.3 65.7 %collective-permute-start.23 = (f32[16,512]{1,0:T(8,128)S(1)}, f32[16,512]{1,0:T(8,128)S(1)}, u32[]{:S(2)}, u32[]{:S(2)}) collective-permute-start(f32[16,512]{1,0:T(8,128)S(1)} %fusion), channel_id=1, source_target_pairs={{0,24},{1,25},{2,26},{3,27},{4,28},{5,29},{6,30},{7,31},{8,32},{9,... | collective-permute-start | bytes 98312
  1329.4 65.7 %collective-permute-start.24 = (f32[16,512]{1,0:T(8,128)S(1)}, f32[16,512]{1,0:T(8,128)S(1)}, u32[]{:S(2)}, u32[]{:S(2)}) collective-permute-start(f32[16,512]{1,0:T(8,128)S(1)} %fusion), channel_id=1, source_target_pairs={{0,25},{1,26},{2,27},{3,28},{4,29},{5,30},{6,31},{7,32},{8,33},{9,... | collective-permute-start | bytes 98312
  1342.6 58.5 %collective-permute-start.25 = (f32[16,512]{1,0:T(8,128)S(1)}, f32[16,512]{1,0:T(8,128)S(1)}, u32[]{:S(2)}, u32[]{:S(2)}) collective-permute-start(f32[16,512]{1,0:T(8,128)S(1)} %fusion), channel_id=1, source_target_pairs={{0,26},{1,27},{2,28},{3,29},{4,30},{5,31},{6,32},{7,33},{8,34},{9,... | collective-permute-start | bytes 98312
  1355.7 56.2 %collective-permute-start.26 = (f32[16,512]{1,0:T(8,128)S(1)}, f32[16,512]{1,0:T(8,128)S(1)}, u32[]{:S(2)}, u32[]{:S(2)}) collective-permute-start(f32[16,512]{1,0:T(8,128)S(1)} %fusion), channel_id=1, source_target_pairs={{0,27},{1,28},{2,29},{3,30},{4,31},{5,32},{6,33},{7,34},{8,35},{9,... | collective-permute-start | bytes 98312
  1368.9 48.7 %collective-permute-start.27 = (f32[16,512]{1,0:T(8,128)S(1)}, f32[16,512]{1,0:T(8,128)S(1)}, u32[]{:S(2)}, u32[]{:S(2)}) collective-permute-start(f32[16,512]{1,0:T(8,128)S(1)} %fusion), channel_id=1, source_target_pairs={{0,28},{1,29},{2,30},{3,31},{4,32},{5,33},{6,34},{7,35},{8,36},{9,... | collective-permute-start | bytes 98312
  1382.0 39.6 %collective-permute-start.28 = (f32[16,512]{1,0:T(8,128)S(1)}, f32[16,512]{1,0:T(8,128)S(1)}, u32[]{:S(2)}, u32[]{:S(2)}) collective-permute-start(f32[16,512]{1,0:T(8,128)S(1)} %fusion), channel_id=1, source_target_pairs={{0,29},{1,30},{2,31},{3,32},{4,33},{5,34},{6,35},{7,36},{8,37},{9,... | collective-permute-start | bytes 98312
  1395.1 28.4 %collective-permute-start.29 = (f32[16,512]{1,0:T(8,128)S(1)}, f32[16,512]{1,0:T(8,128)S(1)}, u32[]{:S(2)}, u32[]{:S(2)}) collective-permute-start(f32[16,512]{1,0:T(8,128)S(1)} %fusion), channel_id=1, source_target_pairs={{0,30},{1,31},{2,32},{3,33},{4,34},{5,35},{6,36},{7,37},{8,38},{9,... | collective-permute-start | bytes 98312
  1401.1 24.3 %collective-permute-start.3 = (f32[16,512]{1,0:T(8,128)S(1)}, f32[16,512]{1,0:T(8,128)S(1)}, u32[]{:S(2)}, u32[]{:S(2)}) collective-permute-start(f32[16,512]{1,0:T(8,128)S(1)} %fusion), channel_id=1, source_target_pairs={{0,4},{1,5},{2,6},{3,7},{4,8},{5,9},{6,10},{7,11},{8,12},{9,13},{1... | collective-permute-start | bytes 98312
  1411.9 15.5 collective-permute-start.30
  1417.6 11.7 collective-permute-start.31
  1421.6 9.7 collective-permute-start.32
  1423.5 9.7 collective-permute-start.33
  1425.5 9.7 collective-permute-start.34
  1427.4 9.7 collective-permute-start.35
  1429.3 32.2 %collective-permute-start.36 = (f32[16,512]{1,0:T(8,128)S(1)}, f32[16,512]{1,0:T(8,128)S(1)}, u32[]{:S(2)}, u32[]{:S(2)}) collective-permute-start(f32[16,512]{1,0:T(8,128)S(1)} %fusion), channel_id=1, source_target_pairs={{0,37},{1,38},{2,39},{3,40},{4,41},{5,42},{6,43},{7,44},{8,45},{9,... | collective-permute-start | bytes 98312
  1431.3 35.2 %collective-permute-start.37 = (f32[16,512]{1,0:T(8,128)S(1)}, f32[16,512]{1,0:T(8,128)S(1)}, u32[]{:S(2)}, u32[]{:S(2)}) collective-permute-start(f32[16,512]{1,0:T(8,128)S(1)} %fusion), channel_id=1, source_target_pairs={{0,38},{1,39},{2,40},{3,41},{4,42},{5,43},{6,44},{7,45},{8,46},{9,... | collective-permute-start | bytes 98312
  1433.2 35.8 %collective-permute-start.38 = (f32[16,512]{1,0:T(8,128)S(1)}, f32[16,512]{1,0:T(8,128)S(1)}, u32[]{:S(2)}, u32[]{:S(2)}) collective-permute-start(f32[16,512]{1,0:T(8,128)S(1)} %fusion), channel_id=1, source_target_pairs={{0,39},{1,40},{2,41},{3,42},{4,43},{5,44},{6,45},{7,46},{8,47},{9,... | collective-permute-start | bytes 98312
  1435.2 35.8 %collective-permute-start.39 = (f32[16,512]{1,0:T(8,128)S(1)}, f32[16,512]{1,0:T(8,128)S(1)}, u32[]{:S(2)}, u32[]{:S(2)}) collective-permute-start(f32[16,512]{1,0:T(8,128)S(1)} %fusion), channel_id=1, source_target_pairs={{0,40},{1,41},{2,42},{3,43},{4,44},{5,45},{6,46},{7,47},{8,48},{9,... | collective-permute-start | bytes 98312
  1437.1 36.1 %collective-permute-start.4 = (f32[16,512]{1,0:T(8,128)S(1)}, f32[16,512]{1,0:T(8,128)S(1)}, u32[]{:S(2)}, u32[]{:S(2)}) collective-permute-start(f32[16,512]{1,0:T(8,128)S(1)} %fusion), channel_id=1, source_target_pairs={{0,5},{1,6},{2,7},{3,8},{4,9},{5,10},{6,11},{7,12},{8,13},{9,14},{... | collective-permute-start | bytes 98312
  1461.6 13.6 collective-permute-start.40
  1466.5 11.1 collective-permute-start.41
  1469.0 10.5 collective-permute-start.42
  1471.0 10.5 collective-permute-start.43
  1473.2 10.2 collective-permute-start.44
  1475.2 10.2 collective-permute-start.45
  1477.6 28.6 %collective-permute-start.46 = (f32[16,512]{1,0:T(8,128)S(1)}, f32[16,512]{1,0:T(8,128)S(1)}, u32[]{:S(2)}, u32[]{:S(2)}) collective-permute-start(f32[16,512]{1,0:T(8,128)S(1)} %fusion), channel_id=1, source_target_pairs={{0,47},{1,48},{2,49},{3,50},{4,51},{5,52},{6,53},{7,54},{8,55},{9,... | collective-permute-start | bytes 98312
  1479.5 32.0 %collective-permute-start.47 = (f32[16,512]{1,0:T(8,128)S(1)}, f32[16,512]{1,0:T(8,128)S(1)}, u32[]{:S(2)}, u32[]{:S(2)}) collective-permute-start(f32[16,512]{1,0:T(8,128)S(1)} %fusion), channel_id=1, source_target_pairs={{0,48},{1,49},{2,50},{3,51},{4,52},{5,53},{6,54},{7,55},{8,56},{9,... | collective-permute-start | bytes 98312
  1481.5 33.3 %collective-permute-start.48 = (f32[16,512]{1,0:T(8,128)S(1)}, f32[16,512]{1,0:T(8,128)S(1)}, u32[]{:S(2)}, u32[]{:S(2)}) collective-permute-start(f32[16,512]{1,0:T(8,128)S(1)} %fusion), channel_id=1, source_target_pairs={{0,49},{1,50},{2,51},{3,52},{4,53},{5,54},{6,55},{7,56},{8,57},{9,... | collective-permute-start | bytes 98312
  1483.4 33.3 %collective-permute-start.49 = (f32[16,512]{1,0:T(8,128)S(1)}, f32[16,512]{1,0:T(8,128)S(1)}, u32[]{:S(2)}, u32[]{:S(2)}) collective-permute-start(f32[16,512]{1,0:T(8,128)S(1)} %fusion), channel_id=1, source_target_pairs={{0,50},{1,51},{2,52},{3,53},{4,54},{5,55},{6,56},{7,57},{8,58},{9,... | collective-permute-start | bytes 98312
  1485.3 33.3 %collective-permute-start.5 = (f32[16,512]{1,0:T(8,128)S(1)}, f32[16,512]{1,0:T(8,128)S(1)}, u32[]{:S(2)}, u32[]{:S(2)}) collective-permute-start(f32[16,512]{1,0:T(8,128)S(1)} %fusion), channel_id=1, source_target_pairs={{0,6},{1,7},{2,8},{3,9},{4,10},{5,11},{6,12},{7,13},{8,14},{9,15},... | collective-permute-start | bytes 98312
  1506.2 14.3 collective-permute-start.50
  1511.6 10.9 collective-permute-start.51
  1514.7 9.7 collective-permute-start.52
  1516.7 9.7 collective-permute-start.53
  1518.6 9.7 collective-permute-start.54
  1520.6 9.7 collective-permute-start.55
  1522.5 25.1 %collective-permute-start.56 = (f32[16,512]{1,0:T(8,128)S(1)}, f32[16,512]{1,0:T(8,128)S(1)}, u32[]{:S(2)}, u32[]{:S(2)}) collective-permute-start(f32[16,512]{1,0:T(8,128)S(1)} %fusion), channel_id=1, source_target_pairs={{0,57},{1,58},{2,59},{3,60},{4,61},{5,62},{6,63},{7,64},{8,65},{9,... | collective-permute-start | bytes 98312
  1524.5 29.6 %collective-permute-start.57 = (f32[16,512]{1,0:T(8,128)S(1)}, f32[16,512]{1,0:T(8,128)S(1)}, u32[]{:S(2)}, u32[]{:S(2)}) collective-permute-start(f32[16,512]{1,0:T(8,128)S(1)} %fusion), channel_id=1, source_target_pairs={{0,58},{1,59},{2,60},{3,61},{4,62},{5,63},{6,64},{7,65},{8,66},{9,... | collective-permute-start | bytes 98312
  1526.4 29.6 %collective-permute-start.58 = (f32[16,512]{1,0:T(8,128)S(1)}, f32[16,512]{1,0:T(8,128)S(1)}, u32[]{:S(2)}, u32[]{:S(2)}) collective-permute-start(f32[16,512]{1,0:T(8,128)S(1)} %fusion), channel_id=1, source_target_pairs={{0,59},{1,60},{2,61},{3,62},{4,63},{5,64},{6,65},{7,66},{8,67},{9,... | collective-permute-start | bytes 98312
  1528.4 29.6 %collective-permute-start.59 = (f32[16,512]{1,0:T(8,128)S(1)}, f32[16,512]{1,0:T(8,128)S(1)}, u32[]{:S(2)}, u32[]{:S(2)}) collective-permute-start(f32[16,512]{1,0:T(8,128)S(1)} %fusion), channel_id=1, source_target_pairs={{0,60},{1,61},{2,62},{3,63},{4,64},{5,65},{6,66},{7,67},{8,68},{9,... | collective-permute-start | bytes 98312
  1530.3 40.4 %collective-permute-start.6 = (f32[16,512]{1,0:T(8,128)S(1)}, f32[16,512]{1,0:T(8,128)S(1)}, u32[]{:S(2)}, u32[]{:S(2)}) collective-permute-start(f32[16,512]{1,0:T(8,128)S(1)} %fusion), channel_id=1, source_target_pairs={{0,7},{1,8},{2,9},{3,10},{4,11},{5,12},{6,13},{7,14},{8,15},{9,16}... | collective-permute-start | bytes 98312
  1547.6 36.2 %collective-permute-start.60 = (f32[16,512]{1,0:T(8,128)S(1)}, f32[16,512]{1,0:T(8,128)S(1)}, u32[]{:S(2)}, u32[]{:S(2)}) collective-permute-start(f32[16,512]{1,0:T(8,128)S(1)} %fusion), channel_id=1, source_target_pairs={{0,61},{1,62},{2,63},{3,64},{4,65},{5,66},{6,67},{7,68},{8,69},{9,... | collective-permute-start | bytes 98312
  1554.1 43.2 %collective-permute-start.61 = (f32[16,512]{1,0:T(8,128)S(1)}, f32[16,512]{1,0:T(8,128)S(1)}, u32[]{:S(2)}, u32[]{:S(2)}) collective-permute-start(f32[16,512]{1,0:T(8,128)S(1)} %fusion), channel_id=1, source_target_pairs={{0,62},{1,63},{2,64},{3,65},{4,66},{5,67},{6,68},{7,69},{8,70},{9,... | collective-permute-start | bytes 98312
  1556.1 41.3 %collective-permute-start.62 = (f32[16,512]{1,0:T(8,128)S(1)}, f32[16,512]{1,0:T(8,128)S(1)}, u32[]{:S(2)}, u32[]{:S(2)}) collective-permute-start(f32[16,512]{1,0:T(8,128)S(1)} %fusion), channel_id=1, source_target_pairs={{0,63},{1,64},{2,65},{3,66},{4,67},{5,68},{6,69},{7,70},{8,71},{9,... | collective-permute-start | bytes 98312
  1558.0 39.3 %collective-permute-start.7 = (f32[16,512]{1,0:T(8,128)S(1)}, f32[16,512]{1,0:T(8,128)S(1)}, u32[]{:S(2)}, u32[]{:S(2)}) collective-permute-start(f32[16,512]{1,0:T(8,128)S(1)} %fusion), channel_id=1, source_target_pairs={{0,8},{1,9},{2,10},{3,11},{4,12},{5,13},{6,14},{7,15},{8,16},{9,17... | collective-permute-start | bytes 98312
  1570.7 26.7 %collective-permute-start.8 = (f32[16,512]{1,0:T(8,128)S(1)}, f32[16,512]{1,0:T(8,128)S(1)}, u32[]{:S(2)}, u32[]{:S(2)}) collective-permute-start(f32[16,512]{1,0:T(8,128)S(1)} %fusion), channel_id=1, source_target_pairs={{0,9},{1,10},{2,11},{3,12},{4,13},{5,14},{6,15},{7,16},{8,17},{9,1... | collective-permute-start | bytes 98312
  1583.9 21.7 %collective-permute-start.9 = (f32[16,512]{1,0:T(8,128)S(1)}, f32[16,512]{1,0:T(8,128)}, u32[]{:S(2)}, u32[]{:S(2)}) collective-permute-start(f32[16,512]{1,0:T(8,128)S(1)} %fusion), channel_id=1, source_target_pairs={{0,10},{1,11},{2,12},{3,13},{4,14},{5,15},{6,16},{7,17},{8,18},{9,... | collective-permute-start | bytes 98312
  (28 other events, 1706.0 us)
where the time goes:
time: 1630 us
  blocking collectives  954 us (59%)
  starting transfers between devices  565 us (35%)
  other arithmetic  59.6 us (4%)
  local copies, waits for them, and re-layouts  26 us (2%)
    unnamed x1, blocking collectives  647 us
    unnamed x64, starting transfers between devices  565 us
    all_gather x1, blocking collectives, on_device(): all_points = lax.all_gather(local_points, ('ga', 'orb'), axis=1, tiled=True)  307 us
    convert_element_type x6, other arithmetic, add_panel(): jnp.cos(angle).astype(jnp.bfloat16)  55.8 us
  transfers between devices with their start and end apart: 64, of which 1 were waited for; matrix products, arithmetic and copies ran while one was open for 0% of the time, Pallas kernels for 0%

commit v1 on v0

--- a/solution.py
+++ b/solution.py
@@ -48,7 +48,8 @@
     coefficients, triples, elec_pos, ion_pos, assignment, rotation, quad_table, inverse_rows
 ):
     local_points = point_coords(elec_pos, ion_pos, assignment, rotation, quad_table)
-    all_points = lax.all_gather(local_points, ("ga", "orb"), axis=1, tiled=True)
+    sent = jnp.stack([local_points] * lax.axis_size(("ga", "orb")))
+    all_points = jnp.concatenate(lax.all_to_all(sent, ("ga", "orb"), 0, 0), axis=1)
     electrons = inverse_rows.shape[0]
     values = lax.psum_scatter(
         phase_values(all_points, triples, coefficients),

time: 1630 us -> 1310 us (0.80)
  blocking collectives: 954 us -> 610 us
    all_gather x1 -> x0, blocking collectives: 307 us -> none  [on_device(): all_points = lax.all_gather(local_points, ('ga', 'orb'), axis=1, tiled=True)]
    unnamed x1, blocking collectives: 647 us -> 610 us
  transfers between devices with their start and end apart: 64 -> 65, of which waited for: 1 -> 2; matrix products, arithmetic and copies ran while one was open for 0% -> 0% of each run, Pallas kernels for 0% -> 0%
where the time goes in v1:
time: 1310 us
  blocking collectives  610 us (47%)
  starting transfers between devices  572 us (44%)
  other arithmetic  59.6 us (5%)
  local copies, waits for them, and re-layouts  26.9 us (2%)
  waiting for transfers between devices  22.7 us (2%)
  matrix products  14.3 us (1%)
    unnamed x1, blocking collectives  610 us
    unnamed x64, starting transfers between devices  558 us
    convert_element_type x6, other arithmetic, add_panel(): jnp.cos(angle).astype(jnp.bfloat16)  55.8 us
  transfers between devices with their start and end apart: 65, of which 2 were waited for; matrix products, arithmetic and copies ran while one was open for 0% of the time, Pallas kernels for 0%

profile of v1, /device:TPU:192, one launch (start us, length us, event | category | flops | bytes accessed | tf_op | source)
XLA Modules:
  0.0 1309.0 jit_solution(4269359673316474000)
XLA Ops:
  6.0 13.5 %all-to-all-start = ((f32[256,3,12]{2,1,0:T(4,128)}), f32[256,3,12]{2,1,0:T(4,128)S(1)}, u32[]{:S(2)}, u32[]{:S(2)}) async-start(f32[256,3,12]{2,1,0:T(4,128)} %stack.3), calls=%async_computation | async-start | bytes 1048576 | tf_op jit(solution)/shard_map/all_to_all | solution.py:52
  20.2 15.6 %all-to-all-done = f32[256,3,12]{2,1,0:T(4,128)S(1)} async-done(((f32[256,3,12]{2,1,0:T(4,128)}), f32[256,3,12]{2,1,0:T(4,128)S(1)}, u32[]{:S(2)}, u32[]{:S(2)}) %all-to-all-start) | async-done | bytes 36896 | tf_op jit(solution)/shard_map/all_to_all | solution.py:52
  36.1 70.7 %while.16 = (s32[]{:T(128)}, f32[6,512,512]{2,1,0:T(8,128)}, f32[6,3,512]{2,0,1:T(8,128)S(1)}, f32[3,1152]{1,0:T(4,128)S(1)}, bf16[2,1152,512]{2,1,0:T(8,128)(2,1)}, /*index=5*/s32[]{:T(128)}, s32[]{:T(128)}, s32[]{}, s32[]{}) while((s32[]{:T(128)}, f32[6,512,512]{2,1,0:T(8,128)}, f32[6,3,512]{2,0,1:T(8,128)S(1)}, f32[3,1152]{1,0:T(4,128)S(1)}, ...), condition=%wide.region_2.3_spmd, body=%wide.region_1.2_spmd.sunk | while | flops 1216806912 | bytes 17624220 | solution.py:44
  36.2 9.3 cosine_convert_fusion.2
  45.5 2.4 fusion.22
  48.0 9.3 cosine_convert_fusion.2
  57.3 2.4 fusion.22
  59.8 9.3 cosine_convert_fusion.2
  69.1 2.4 fusion.22
  71.5 9.3 cosine_convert_fusion.2
  80.9 2.4 fusion.22
  83.3 9.3 cosine_convert_fusion.2
  92.6 2.4 fusion.22
  95.1 9.3 cosine_convert_fusion.2
  104.4 2.4 fusion.22
  106.8 610.4 %fusion = f32[16,512]{1,0:T(8,128)S(1)} fusion(f32[3072,512]{1,0:T(8,128)} %bitcast.36), kind=kCustom, calls=%all-reduce-scatter | all-reduce-scatter fusion | flops 2097153 | bytes 6324224
  717.2 85.6 %collective-permute-start = (f32[16,512]{1,0:T(8,128)S(1)}, f32[16,512]{1,0:T(8,128)S(1)}, u32[]{:S(2)}, u32[]{:S(2)}) collective-permute-start(f32[16,512]{1,0:T(8,128)S(1)} %fusion), channel_id=1, source_target_pairs={{0,1},{1,2},{2,3},{3,4},{4,5},{5,6},{6,7},{7,8},{8,9},{9,10},{10,1... | collective-permute-start | bytes 98312
  802.8 13.1 %collective-permute-start.1 = (f32[16,512]{1,0:T(8,128)S(1)}, f32[16,512]{1,0:T(8,128)S(1)}, u32[]{:S(2)}, u32[]{:S(2)}) collective-permute-start(f32[16,512]{1,0:T(8,128)S(1)} %fusion), channel_id=1, source_target_pairs={{0,2},{1,3},{2,4},{3,5},{4,6},{5,7},{6,8},{7,9},{8,10},{9,11},{10,... | collective-permute-start | bytes 98312
  816.0 13.1 %collective-permute-start.10 = (f32[16,512]{1,0:T(8,128)S(1)}, f32[16,512]{1,0:T(8,128)S(1)}, u32[]{:S(2)}, u32[]{:S(2)}) collective-permute-start(f32[16,512]{1,0:T(8,128)S(1)} %fusion), channel_id=1, source_target_pairs={{0,11},{1,12},{2,13},{3,14},{4,15},{5,16},{6,17},{7,18},{8,19},{9,... | collective-permute-start | bytes 98312
  830.4 14.8 %collective-permute-start.11 = (f32[16,512]{1,0:T(8,128)S(1)}, f32[16,512]{1,0:T(8,128)S(1)}, u32[]{:S(2)}, u32[]{:S(2)}) collective-permute-start(f32[16,512]{1,0:T(8,128)S(1)} %fusion), channel_id=1, source_target_pairs={{0,12},{1,13},{2,14},{3,15},{4,16},{5,17},{6,18},{7,19},{8,20},{9,... | collective-permute-start | bytes 98312
  845.3 13.1 %collective-permute-start.12 = (f32[16,512]{1,0:T(8,128)S(1)}, f32[16,512]{1,0:T(8,128)S(1)}, u32[]{:S(2)}, u32[]{:S(2)}) collective-permute-start(f32[16,512]{1,0:T(8,128)S(1)} %fusion), channel_id=1, source_target_pairs={{0,13},{1,14},{2,15},{3,16},{4,17},{5,18},{6,19},{7,20},{8,21},{9,... | collective-permute-start | bytes 98312
  858.4 13.1 %collective-permute-start.13 = (f32[16,512]{1,0:T(8,128)S(1)}, f32[16,512]{1,0:T(8,128)S(1)}, u32[]{:S(2)}, u32[]{:S(2)}) collective-permute-start(f32[16,512]{1,0:T(8,128)S(1)} %fusion), channel_id=1, source_target_pairs={{0,14},{1,15},{2,16},{3,17},{4,18},{5,19},{6,20},{7,21},{8,22},{9,... | collective-permute-start | bytes 98312
  871.5 13.1 %collective-permute-start.14 = (f32[16,512]{1,0:T(8,128)S(1)}, f32[16,512]{1,0:T(8,128)S(1)}, u32[]{:S(2)}, u32[]{:S(2)}) collective-permute-start(f32[16,512]{1,0:T(8,128)S(1)} %fusion), channel_id=1, source_target_pairs={{0,15},{1,16},{2,17},{3,18},{4,19},{5,20},{6,21},{7,22},{8,23},{9,... | collective-permute-start | bytes 98312
  884.7 13.1 %collective-permute-start.15 = (f32[16,512]{1,0:T(8,128)S(1)}, f32[16,512]{1,0:T(8,128)S(1)}, u32[]{:S(2)}, u32[]{:S(2)}) collective-permute-start(f32[16,512]{1,0:T(8,128)S(1)} %fusion), channel_id=1, source_target_pairs={{0,16},{1,17},{2,18},{3,19},{4,20},{5,21},{6,22},{7,23},{8,24},{9,... | collective-permute-start | bytes 98312
  897.8 13.1 %collective-permute-start.16 = (f32[16,512]{1,0:T(8,128)S(1)}, f32[16,512]{1,0:T(8,128)S(1)}, u32[]{:S(2)}, u32[]{:S(2)}) collective-permute-start(f32[16,512]{1,0:T(8,128)S(1)} %fusion), channel_id=1, source_target_pairs={{0,17},{1,18},{2,19},{3,20},{4,21},{5,22},{6,23},{7,24},{8,25},{9,... | collective-permute-start | bytes 98312
  911.0 13.1 %collective-permute-start.17 = (f32[16,512]{1,0:T(8,128)S(1)}, f32[16,512]{1,0:T(8,128)S(1)}, u32[]{:S(2)}, u32[]{:S(2)}) collective-permute-start(f32[16,512]{1,0:T(8,128)S(1)} %fusion), channel_id=1, source_target_pairs={{0,18},{1,19},{2,20},{3,21},{4,22},{5,23},{6,24},{7,25},{8,26},{9,... | collective-permute-start | bytes 98312
  924.1 13.1 %collective-permute-start.18 = (f32[16,512]{1,0:T(8,128)S(1)}, f32[16,512]{1,0:T(8,128)S(1)}, u32[]{:S(2)}, u32[]{:S(2)}) collective-permute-start(f32[16,512]{1,0:T(8,128)S(1)} %fusion), channel_id=1, source_target_pairs={{0,19},{1,20},{2,21},{3,22},{4,23},{5,24},{6,25},{7,26},{8,27},{9,... | collective-permute-start | bytes 98312
  937.2 13.1 %collective-permute-start.19 = (f32[16,512]{1,0:T(8,128)S(1)}, f32[16,512]{1,0:T(8,128)S(1)}, u32[]{:S(2)}, u32[]{:S(2)}) collective-permute-start(f32[16,512]{1,0:T(8,128)S(1)} %fusion), channel_id=1, source_target_pairs={{0,20},{1,21},{2,22},{3,23},{4,24},{5,25},{6,26},{7,27},{8,28},{9,... | collective-permute-start | bytes 98312
  950.4 13.1 %collective-permute-start.2 = (f32[16,512]{1,0:T(8,128)S(1)}, f32[16,512]{1,0:T(8,128)S(1)}, u32[]{:S(2)}, u32[]{:S(2)}) collective-permute-start(f32[16,512]{1,0:T(8,128)S(1)} %fusion), channel_id=1, source_target_pairs={{0,3},{1,4},{2,5},{3,6},{4,7},{5,8},{6,9},{7,10},{8,11},{9,12},{10... | collective-permute-start | bytes 98312
  963.5 13.1 %collective-permute-start.20 = (f32[16,512]{1,0:T(8,128)S(1)}, f32[16,512]{1,0:T(8,128)S(1)}, u32[]{:S(2)}, u32[]{:S(2)}) collective-permute-start(f32[16,512]{1,0:T(8,128)S(1)} %fusion), channel_id=1, source_target_pairs={{0,21},{1,22},{2,23},{3,24},{4,25},{5,26},{6,27},{7,28},{8,29},{9,... | collective-permute-start | bytes 98312
  976.7 13.1 %collective-permute-start.21 = (f32[16,512]{1,0:T(8,128)S(1)}, f32[16,512]{1,0:T(8,128)S(1)}, u32[]{:S(2)}, u32[]{:S(2)}) collective-permute-start(f32[16,512]{1,0:T(8,128)S(1)} %fusion), channel_id=1, source_target_pairs={{0,22},{1,23},{2,24},{3,25},{4,26},{5,27},{6,28},{7,29},{8,30},{9,... | collective-permute-start | bytes 98312
  989.8 13.1 %collective-permute-start.22 = (f32[16,512]{1,0:T(8,128)S(1)}, f32[16,512]{1,0:T(8,128)S(1)}, u32[]{:S(2)}, u32[]{:S(2)}) collective-permute-start(f32[16,512]{1,0:T(8,128)S(1)} %fusion), channel_id=1, source_target_pairs={{0,23},{1,24},{2,25},{3,26},{4,27},{5,28},{6,29},{7,30},{8,31},{9,... | collective-permute-start | bytes 98312
  1002.9 13.1 %collective-permute-start.23 = (f32[16,512]{1,0:T(8,128)S(1)}, f32[16,512]{1,0:T(8,128)S(1)}, u32[]{:S(2)}, u32[]{:S(2)}) collective-permute-start(f32[16,512]{1,0:T(8,128)S(1)} %fusion), channel_id=1, source_target_pairs={{0,24},{1,25},{2,26},{3,27},{4,28},{5,29},{6,30},{7,31},{8,32},{9,... | collective-permute-start | bytes 98312
  1016.1 13.1 %collective-permute-start.24 = (f32[16,512]{1,0:T(8,128)S(1)}, f32[16,512]{1,0:T(8,128)S(1)}, u32[]{:S(2)}, u32[]{:S(2)}) collective-permute-start(f32[16,512]{1,0:T(8,128)S(1)} %fusion), channel_id=1, source_target_pairs={{0,25},{1,26},{2,27},{3,28},{4,29},{5,30},{6,31},{7,32},{8,33},{9,... | collective-permute-start | bytes 98312
  1029.2 13.1 %collective-permute-start.25 = (f32[16,512]{1,0:T(8,128)S(1)}, f32[16,512]{1,0:T(8,128)S(1)}, u32[]{:S(2)}, u32[]{:S(2)}) collective-permute-start(f32[16,512]{1,0:T(8,128)S(1)} %fusion), channel_id=1, source_target_pairs={{0,26},{1,27},{2,28},{3,29},{4,30},{5,31},{6,32},{7,33},{8,34},{9,... | collective-permute-start | bytes 98312
  1042.4 13.1 %collective-permute-start.26 = (f32[16,512]{1,0:T(8,128)S(1)}, f32[16,512]{1,0:T(8,128)S(1)}, u32[]{:S(2)}, u32[]{:S(2)}) collective-permute-start(f32[16,512]{1,0:T(8,128)S(1)} %fusion), channel_id=1, source_target_pairs={{0,27},{1,28},{2,29},{3,30},{4,31},{5,32},{6,33},{7,34},{8,35},{9,... | collective-permute-start | bytes 98312
  1055.5 13.1 %collective-permute-start.27 = (f32[16,512]{1,0:T(8,128)S(1)}, f32[16,512]{1,0:T(8,128)S(1)}, u32[]{:S(2)}, u32[]{:S(2)}) collective-permute-start(f32[16,512]{1,0:T(8,128)S(1)} %fusion), channel_id=1, source_target_pairs={{0,28},{1,29},{2,30},{3,31},{4,32},{5,33},{6,34},{7,35},{8,36},{9,... | collective-permute-start | bytes 98312
  1068.6 5.9 collective-permute-start.28
  1074.6 3.9 collective-permute-start.29
  1078.5 12.9 collective-permute-start.3
  1091.4 5.7 collective-permute-start.30
  1097.1 3.9 collective-permute-start.31
  1103.0 1.9 collective-permute-start.33
  1112.7 1.9 collective-permute-start.38
  1116.6 24.4 %collective-permute-start.4 = (f32[16,512]{1,0:T(8,128)S(1)}, f32[16,512]{1,0:T(8,128)S(1)}, u32[]{:S(2)}, u32[]{:S(2)}) collective-permute-start(f32[16,512]{1,0:T(8,128)S(1)} %fusion), channel_id=1, source_target_pairs={{0,5},{1,6},{2,7},{3,8},{4,9},{5,10},{6,11},{7,12},{8,13},{9,14},{... | collective-permute-start | bytes 98312
  1141.0 4.9 collective-permute-start.40
  1145.9 2.5 collective-permute-start.41
  1150.4 2.2 collective-permute-start.43
  1152.7 1.9 collective-permute-start.44
  1154.6 2.4 collective-permute-start.45
  1157.0 1.9 collective-permute-start.46
  1162.9 1.9 collective-permute-start.49
  1164.8 20.8 %collective-permute-start.5 = (f32[16,512]{1,0:T(8,128)S(1)}, f32[16,512]{1,0:T(8,128)S(1)}, u32[]{:S(2)}, u32[]{:S(2)}) collective-permute-start(f32[16,512]{1,0:T(8,128)S(1)} %fusion), channel_id=1, source_target_pairs={{0,6},{1,7},{2,8},{3,9},{4,10},{5,11},{6,12},{7,13},{8,14},{9,15},... | collective-permute-start | bytes 98312
  1185.7 5.3 collective-permute-start.50
  1191.0 3.1 collective-permute-start.51
  1196.1 1.9 collective-permute-start.53
  1200.0 1.9 collective-permute-start.55
  1209.8 17.3 %collective-permute-start.6 = (f32[16,512]{1,0:T(8,128)S(1)}, f32[16,512]{1,0:T(8,128)S(1)}, u32[]{:S(2)}, u32[]{:S(2)}) collective-permute-start(f32[16,512]{1,0:T(8,128)S(1)} %fusion), channel_id=1, source_target_pairs={{0,7},{1,8},{2,9},{3,10},{4,11},{5,12},{6,13},{7,14},{8,15},{9,16}... | collective-permute-start | bytes 98312
  1227.1 6.5 collective-permute-start.60
  1237.5 12.6 collective-permute-start.7
  1250.2 13.1 %collective-permute-start.8 = (f32[16,512]{1,0:T(8,128)S(1)}, f32[16,512]{1,0:T(8,128)S(1)}, u32[]{:S(2)}, u32[]{:S(2)}) collective-permute-start(f32[16,512]{1,0:T(8,128)S(1)} %fusion), channel_id=1, source_target_pairs={{0,9},{1,10},{2,11},{3,12},{4,13},{5,14},{6,15},{7,16},{8,17},{9,1... | collective-permute-start | bytes 98312
  1263.3 13.3 %collective-permute-start.9 = (f32[16,512]{1,0:T(8,128)S(1)}, f32[16,512]{1,0:T(8,128)}, u32[]{:S(2)}, u32[]{:S(2)}) collective-permute-start(f32[16,512]{1,0:T(8,128)S(1)} %fusion), channel_id=1, source_target_pairs={{0,10},{1,11},{2,12},{3,13},{4,14},{5,15},{6,16},{7,17},{8,18},{9,... | collective-permute-start | bytes 98312
  1278.1 6.9 collective-permute-done.9
  1285.0 23.3 %concatenate.6 = f32[1036,512]{1,0:T(8,128)S(1)} concatenate(f32[12,512]{1,0:T(8,128)S(1)} %collective-permute-done.63, f32[16,512]{1,0:T(8,128)} %copy-done.18, f32[16,512]{1,0:T(8,128)} %copy-done.17, f32[16,512]{1,0:T(8,128)} %copy-done.16, f32[16,512]{1,0:T(8,128)} %copy-done.14, f32[16,512]{1,0:T(8,128)} %copy-done.13, f32[16,512]{1,0:T(8,128)} %copy-done.12, ...), dimensions={0} | concatenate | bytes 4243456
  (160 shorter events, 41.4 us)
Async XLA Ops:
  6.0 29.8 %all-to-all-start = ((f32[256,3,12]{2,1,0:T(4,128)}), f32[256,3,12]{2,1,0:T(4,128)S(1)}, u32[]{:S(2)}, u32[]{:S(2)}) async-start(f32[256,3,12]{2,1,0:T(4,128)} %stack.3), calls=%async_computation | async-start | bytes 1048576 | tf_op jit(solution)/shard_map/all_to_all | solution.py:52
  717.2 141.2 %collective-permute-start = (f32[16,512]{1,0:T(8,128)S(1)}, f32[16,512]{1,0:T(8,128)S(1)}, u32[]{:S(2)}, u32[]{:S(2)}) collective-permute-start(f32[16,512]{1,0:T(8,128)S(1)} %fusion), channel_id=1, source_target_pairs={{0,1},{1,2},{2,3},{3,4},{4,5},{5,6},{6,7},{7,8},{8,9},{9,10},{10,1... | collective-permute-start | bytes 98312
  802.8 68.7 %collective-permute-start.1 = (f32[16,512]{1,0:T(8,128)S(1)}, f32[16,512]{1,0:T(8,128)S(1)}, u32[]{:S(2)}, u32[]{:S(2)}) collective-permute-start(f32[16,512]{1,0:T(8,128)S(1)} %fusion), channel_id=1, source_target_pairs={{0,2},{1,3},{2,4},{3,5},{4,6},{5,7},{6,8},{7,9},{8,10},{9,11},{10,... | collective-permute-start | bytes 98312
  816.0 68.7 %collective-permute-start.10 = (f32[16,512]{1,0:T(8,128)S(1)}, f32[16,512]{1,0:T(8,128)S(1)}, u32[]{:S(2)}, u32[]{:S(2)}) collective-permute-start(f32[16,512]{1,0:T(8,128)S(1)} %fusion), channel_id=1, source_target_pairs={{0,11},{1,12},{2,13},{3,14},{4,15},{5,16},{6,17},{7,18},{8,19},{9,... | collective-permute-start | bytes 98312
  829.1 16.2 %collective-permute-start.63 = (f32[12,512]{1,0:T(8,128)S(1)}, f32[12,512]{1,0:T(8,128)S(1)}, u32[]{:S(2)}, u32[]{:S(2)}) collective-permute-start(f32[12,512]{1,0:T(8,128)S(1)} %slice.43), channel_id=1, source_target_pairs={{0,64},{1,65},{2,66},{3,67},{4,68},{5,69},{6,70},{7,71},{8,72},{9,... | collective-permute-start | bytes 73736
  830.4 67.4 %collective-permute-start.11 = (f32[16,512]{1,0:T(8,128)S(1)}, f32[16,512]{1,0:T(8,128)S(1)}, u32[]{:S(2)}, u32[]{:S(2)}) collective-permute-start(f32[16,512]{1,0:T(8,128)S(1)} %fusion), channel_id=1, source_target_pairs={{0,12},{1,13},{2,14},{3,15},{4,16},{5,17},{6,18},{7,19},{8,20},{9,... | collective-permute-start | bytes 98312
  845.3 65.7 %collective-permute-start.12 = (f32[16,512]{1,0:T(8,128)S(1)}, f32[16,512]{1,0:T(8,128)S(1)}, u32[]{:S(2)}, u32[]{:S(2)}) collective-permute-start(f32[16,512]{1,0:T(8,128)S(1)} %fusion), channel_id=1, source_target_pairs={{0,13},{1,14},{2,15},{3,16},{4,17},{5,18},{6,19},{7,20},{8,21},{9,... | collective-permute-start | bytes 98312
  858.4 65.7 %collective-permute-start.13 = (f32[16,512]{1,0:T(8,128)S(1)}, f32[16,512]{1,0:T(8,128)S(1)}, u32[]{:S(2)}, u32[]{:S(2)}) collective-permute-start(f32[16,512]{1,0:T(8,128)S(1)} %fusion), channel_id=1, source_target_pairs={{0,14},{1,15},{2,16},{3,17},{4,18},{5,19},{6,20},{7,21},{8,22},{9,... | collective-permute-start | bytes 98312
  871.5 65.7 %collective-permute-start.14 = (f32[16,512]{1,0:T(8,128)S(1)}, f32[16,512]{1,0:T(8,128)S(1)}, u32[]{:S(2)}, u32[]{:S(2)}) collective-permute-start(f32[16,512]{1,0:T(8,128)S(1)} %fusion), channel_id=1, source_target_pairs={{0,15},{1,16},{2,17},{3,18},{4,19},{5,20},{6,21},{7,22},{8,23},{9,... | collective-permute-start | bytes 98312
  884.7 65.7 %collective-permute-start.15 = (f32[16,512]{1,0:T(8,128)S(1)}, f32[16,512]{1,0:T(8,128)S(1)}, u32[]{:S(2)}, u32[]{:S(2)}) collective-permute-start(f32[16,512]{1,0:T(8,128)S(1)} %fusion), channel_id=1, source_target_pairs={{0,16},{1,17},{2,18},{3,19},{4,20},{5,21},{6,22},{7,23},{8,24},{9,... | collective-permute-start | bytes 98312
  897.8 65.7 %collective-permute-start.16 = (f32[16,512]{1,0:T(8,128)S(1)}, f32[16,512]{1,0:T(8,128)S(1)}, u32[]{:S(2)}, u32[]{:S(2)}) collective-permute-start(f32[16,512]{1,0:T(8,128)S(1)} %fusion), channel_id=1, source_target_pairs={{0,17},{1,18},{2,19},{3,20},{4,21},{5,22},{6,23},{7,24},{8,25},{9,... | collective-permute-start | bytes 98312
  911.0 65.7 %collective-permute-start.17 = (f32[16,512]{1,0:T(8,128)S(1)}, f32[16,512]{1,0:T(8,128)S(1)}, u32[]{:S(2)}, u32[]{:S(2)}) collective-permute-start(f32[16,512]{1,0:T(8,128)S(1)} %fusion), channel_id=1, source_target_pairs={{0,18},{1,19},{2,20},{3,21},{4,22},{5,23},{6,24},{7,25},{8,26},{9,... | collective-permute-start | bytes 98312
  924.1 65.7 %collective-permute-start.18 = (f32[16,512]{1,0:T(8,128)S(1)}, f32[16,512]{1,0:T(8,128)S(1)}, u32[]{:S(2)}, u32[]{:S(2)}) collective-permute-start(f32[16,512]{1,0:T(8,128)S(1)} %fusion), channel_id=1, source_target_pairs={{0,19},{1,20},{2,21},{3,22},{4,23},{5,24},{6,25},{7,26},{8,27},{9,... | collective-permute-start | bytes 98312
  937.2 65.7 %collective-permute-start.19 = (f32[16,512]{1,0:T(8,128)S(1)}, f32[16,512]{1,0:T(8,128)S(1)}, u32[]{:S(2)}, u32[]{:S(2)}) collective-permute-start(f32[16,512]{1,0:T(8,128)S(1)} %fusion), channel_id=1, source_target_pairs={{0,20},{1,21},{2,22},{3,23},{4,24},{5,25},{6,26},{7,27},{8,28},{9,... | collective-permute-start | bytes 98312
  950.4 65.7 %collective-permute-start.2 = (f32[16,512]{1,0:T(8,128)S(1)}, f32[16,512]{1,0:T(8,128)S(1)}, u32[]{:S(2)}, u32[]{:S(2)}) collective-permute-start(f32[16,512]{1,0:T(8,128)S(1)} %fusion), channel_id=1, source_target_pairs={{0,3},{1,4},{2,5},{3,6},{4,7},{5,8},{6,9},{7,10},{8,11},{9,12},{10... | collective-permute-start | bytes 98312
  963.5 65.7 %collective-permute-start.20 = (f32[16,512]{1,0:T(8,128)S(1)}, f32[16,512]{1,0:T(8,128)S(1)}, u32[]{:S(2)}, u32[]{:S(2)}) collective-permute-start(f32[16,512]{1,0:T(8,128)S(1)} %fusion), channel_id=1, source_target_pairs={{0,21},{1,22},{2,23},{3,24},{4,25},{5,26},{6,27},{7,28},{8,29},{9,... | collective-permute-start | bytes 98312
  976.7 65.7 %collective-permute-start.21 = (f32[16,512]{1,0:T(8,128)S(1)}, f32[16,512]{1,0:T(8,128)S(1)}, u32[]{:S(2)}, u32[]{:S(2)}) collective-permute-start(f32[16,512]{1,0:T(8,128)S(1)} %fusion), channel_id=1, source_target_pairs={{0,22},{1,23},{2,24},{3,25},{4,26},{5,27},{6,28},{7,29},{8,30},{9,... | collective-permute-start | bytes 98312
  989.8 65.7 %collective-permute-start.22 = (f32[16,512]{1,0:T(8,128)S(1)}, f32[16,512]{1,0:T(8,128)S(1)}, u32[]{:S(2)}, u32[]{:S(2)}) collective-permute-start(f32[16,512]{1,0:T(8,128)S(1)} %fusion), channel_id=1, source_target_pairs={{0,23},{1,24},{2,25},{3,26},{4,27},{5,28},{6,29},{7,30},{8,31},{9,... | collective-permute-start | bytes 98312
  1002.9 65.7 %collective-permute-start.23 = (f32[16,512]{1,0:T(8,128)S(1)}, f32[16,512]{1,0:T(8,128)S(1)}, u32[]{:S(2)}, u32[]{:S(2)}) collective-permute-start(f32[16,512]{1,0:T(8,128)S(1)} %fusion), channel_id=1, source_target_pairs={{0,24},{1,25},{2,26},{3,27},{4,28},{5,29},{6,30},{7,31},{8,32},{9,... | collective-permute-start | bytes 98312
  1016.1 58.5 %collective-permute-start.24 = (f32[16,512]{1,0:T(8,128)S(1)}, f32[16,512]{1,0:T(8,128)S(1)}, u32[]{:S(2)}, u32[]{:S(2)}) collective-permute-start(f32[16,512]{1,0:T(8,128)S(1)} %fusion), channel_id=1, source_target_pairs={{0,25},{1,26},{2,27},{3,28},{4,29},{5,30},{6,31},{7,32},{8,33},{9,... | collective-permute-start | bytes 98312
  1029.2 49.3 %collective-permute-start.25 = (f32[16,512]{1,0:T(8,128)S(1)}, f32[16,512]{1,0:T(8,128)S(1)}, u32[]{:S(2)}, u32[]{:S(2)}) collective-permute-start(f32[16,512]{1,0:T(8,128)S(1)} %fusion), channel_id=1, source_target_pairs={{0,26},{1,27},{2,28},{3,29},{4,30},{5,31},{6,32},{7,33},{8,34},{9,... | collective-permute-start | bytes 98312
  1042.4 49.0 %collective-permute-start.26 = (f32[16,512]{1,0:T(8,128)S(1)}, f32[16,512]{1,0:T(8,128)S(1)}, u32[]{:S(2)}, u32[]{:S(2)}) collective-permute-start(f32[16,512]{1,0:T(8,128)S(1)} %fusion), channel_id=1, source_target_pairs={{0,27},{1,28},{2,29},{3,30},{4,31},{5,32},{6,33},{7,34},{8,35},{9,... | collective-permute-start | bytes 98312
  1055.5 41.6 %collective-permute-start.27 = (f32[16,512]{1,0:T(8,128)S(1)}, f32[16,512]{1,0:T(8,128)S(1)}, u32[]{:S(2)}, u32[]{:S(2)}) collective-permute-start(f32[16,512]{1,0:T(8,128)S(1)} %fusion), channel_id=1, source_target_pairs={{0,28},{1,29},{2,30},{3,31},{4,32},{5,33},{6,34},{7,35},{8,36},{9,... | collective-permute-start | bytes 98312
  1068.6 32.4 %collective-permute-start.28 = (f32[16,512]{1,0:T(8,128)S(1)}, f32[16,512]{1,0:T(8,128)S(1)}, u32[]{:S(2)}, u32[]{:S(2)}) collective-permute-start(f32[16,512]{1,0:T(8,128)S(1)} %fusion), channel_id=1, source_target_pairs={{0,29},{1,30},{2,31},{3,32},{4,33},{5,34},{6,35},{7,36},{8,37},{9,... | collective-permute-start | bytes 98312
  1074.6 28.4 %collective-permute-start.29 = (f32[16,512]{1,0:T(8,128)S(1)}, f32[16,512]{1,0:T(8,128)S(1)}, u32[]{:S(2)}, u32[]{:S(2)}) collective-permute-start(f32[16,512]{1,0:T(8,128)S(1)} %fusion), channel_id=1, source_target_pairs={{0,30},{1,31},{2,32},{3,33},{4,34},{5,35},{6,36},{7,37},{8,38},{9,... | collective-permute-start | bytes 98312
  1078.5 26.4 %collective-permute-start.3 = (f32[16,512]{1,0:T(8,128)S(1)}, f32[16,512]{1,0:T(8,128)S(1)}, u32[]{:S(2)}, u32[]{:S(2)}) collective-permute-start(f32[16,512]{1,0:T(8,128)S(1)} %fusion), channel_id=1, source_target_pairs={{0,4},{1,5},{2,6},{3,7},{4,8},{5,9},{6,10},{7,11},{8,12},{9,13},{1... | collective-permute-start | bytes 98312
  1091.4 15.5 %collective-permute-start.30 = (f32[16,512]{1,0:T(8,128)S(1)}, f32[16,512]{1,0:T(8,128)S(1)}, u32[]{:S(2)}, u32[]{:S(2)}) collective-permute-start(f32[16,512]{1,0:T(8,128)S(1)} %fusion), channel_id=1, source_target_pairs={{0,31},{1,32},{2,33},{3,34},{4,35},{5,36},{6,37},{7,38},{8,39},{9,... | collective-permute-start | bytes 98312
  1097.1 11.7 collective-permute-start.31
  1101.0 9.7 collective-permute-start.32
  1103.0 9.7 collective-permute-start.33
  1104.9 9.7 collective-permute-start.34
  1108.8 32.2 %collective-permute-start.36 = (f32[16,512]{1,0:T(8,128)S(1)}, f32[16,512]{1,0:T(8,128)S(1)}, u32[]{:S(2)}, u32[]{:S(2)}) collective-permute-start(f32[16,512]{1,0:T(8,128)S(1)} %fusion), channel_id=1, source_target_pairs={{0,37},{1,38},{2,39},{3,40},{4,41},{5,42},{6,43},{7,44},{8,45},{9,... | collective-permute-start | bytes 98312
  1110.7 35.2 %collective-permute-start.37 = (f32[16,512]{1,0:T(8,128)S(1)}, f32[16,512]{1,0:T(8,128)S(1)}, u32[]{:S(2)}, u32[]{:S(2)}) collective-permute-start(f32[16,512]{1,0:T(8,128)S(1)} %fusion), channel_id=1, source_target_pairs={{0,38},{1,39},{2,40},{3,41},{4,42},{5,43},{6,44},{7,45},{8,46},{9,... | collective-permute-start | bytes 98312
  1112.7 35.8 %collective-permute-start.38 = (f32[16,512]{1,0:T(8,128)S(1)}, f32[16,512]{1,0:T(8,128)S(1)}, u32[]{:S(2)}, u32[]{:S(2)}) collective-permute-start(f32[16,512]{1,0:T(8,128)S(1)} %fusion), channel_id=1, source_target_pairs={{0,39},{1,40},{2,41},{3,42},{4,43},{5,44},{6,45},{7,46},{8,47},{9,... | collective-permute-start | bytes 98312
  1114.6 35.8 %collective-permute-start.39 = (f32[16,512]{1,0:T(8,128)S(1)}, f32[16,512]{1,0:T(8,128)S(1)}, u32[]{:S(2)}, u32[]{:S(2)}) collective-permute-start(f32[16,512]{1,0:T(8,128)S(1)} %fusion), channel_id=1, source_target_pairs={{0,40},{1,41},{2,42},{3,43},{4,44},{5,45},{6,46},{7,47},{8,48},{9,... | collective-permute-start | bytes 98312
  1116.6 36.1 %collective-permute-start.4 = (f32[16,512]{1,0:T(8,128)S(1)}, f32[16,512]{1,0:T(8,128)S(1)}, u32[]{:S(2)}, u32[]{:S(2)}) collective-permute-start(f32[16,512]{1,0:T(8,128)S(1)} %fusion), channel_id=1, source_target_pairs={{0,5},{1,6},{2,7},{3,8},{4,9},{5,10},{6,11},{7,12},{8,13},{9,14},{... | collective-permute-start | bytes 98312
  1141.0 13.6 %collective-permute-start.40 = (f32[16,512]{1,0:T(8,128)S(1)}, f32[16,512]{1,0:T(8,128)S(1)}, u32[]{:S(2)}, u32[]{:S(2)}) collective-permute-start(f32[16,512]{1,0:T(8,128)S(1)} %fusion), channel_id=1, source_target_pairs={{0,41},{1,42},{2,43},{3,44},{4,45},{5,46},{6,47},{7,48},{8,49},{9,... | collective-permute-start | bytes 98312
  1145.9 11.1 collective-permute-start.41
  1148.5 10.5 collective-permute-start.42
  1150.4 10.5 collective-permute-start.43
  1152.7 10.2 collective-permute-start.44
  1154.6 10.2 collective-permute-start.45
  1157.0 28.6 %collective-permute-start.46 = (f32[16,512]{1,0:T(8,128)S(1)}, f32[16,512]{1,0:T(8,128)S(1)}, u32[]{:S(2)}, u32[]{:S(2)}) collective-permute-start(f32[16,512]{1,0:T(8,128)S(1)} %fusion), channel_id=1, source_target_pairs={{0,47},{1,48},{2,49},{3,50},{4,51},{5,52},{6,53},{7,54},{8,55},{9,... | collective-permute-start | bytes 98312
  1159.0 32.0 %collective-permute-start.47 = (f32[16,512]{1,0:T(8,128)S(1)}, f32[16,512]{1,0:T(8,128)S(1)}, u32[]{:S(2)}, u32[]{:S(2)}) collective-permute-start(f32[16,512]{1,0:T(8,128)S(1)} %fusion), channel_id=1, source_target_pairs={{0,48},{1,49},{2,50},{3,51},{4,52},{5,53},{6,54},{7,55},{8,56},{9,... | collective-permute-start | bytes 98312
  1160.9 33.3 %collective-permute-start.48 = (f32[16,512]{1,0:T(8,128)S(1)}, f32[16,512]{1,0:T(8,128)S(1)}, u32[]{:S(2)}, u32[]{:S(2)}) collective-permute-start(f32[16,512]{1,0:T(8,128)S(1)} %fusion), channel_id=1, source_target_pairs={{0,49},{1,50},{2,51},{3,52},{4,53},{5,54},{6,55},{7,56},{8,57},{9,... | collective-permute-start | bytes 98312
  1162.9 33.3 %collective-permute-start.49 = (f32[16,512]{1,0:T(8,128)S(1)}, f32[16,512]{1,0:T(8,128)S(1)}, u32[]{:S(2)}, u32[]{:S(2)}) collective-permute-start(f32[16,512]{1,0:T(8,128)S(1)} %fusion), channel_id=1, source_target_pairs={{0,50},{1,51},{2,52},{3,53},{4,54},{5,55},{6,56},{7,57},{8,58},{9,... | collective-permute-start | bytes 98312
  1164.8 33.3 %collective-permute-start.5 = (f32[16,512]{1,0:T(8,128)S(1)}, f32[16,512]{1,0:T(8,128)S(1)}, u32[]{:S(2)}, u32[]{:S(2)}) collective-permute-start(f32[16,512]{1,0:T(8,128)S(1)} %fusion), channel_id=1, source_target_pairs={{0,6},{1,7},{2,8},{3,9},{4,10},{5,11},{6,12},{7,13},{8,14},{9,15},... | collective-permute-start | bytes 98312
  1185.7 14.3 %collective-permute-start.50 = (f32[16,512]{1,0:T(8,128)S(1)}, f32[16,512]{1,0:T(8,128)S(1)}, u32[]{:S(2)}, u32[]{:S(2)}) collective-permute-start(f32[16,512]{1,0:T(8,128)S(1)} %fusion), channel_id=1, source_target_pairs={{0,51},{1,52},{2,53},{3,54},{4,55},{5,56},{6,57},{7,58},{8,59},{9,... | collective-permute-start | bytes 98312
  1191.0 10.9 collective-permute-start.51
  1194.2 9.7 collective-permute-start.52
  1196.1 9.7 collective-permute-start.53
  1198.1 9.7 collective-permute-start.54
  1200.0 9.7 collective-permute-start.55
  1202.0 25.1 %collective-permute-start.56 = (f32[16,512]{1,0:T(8,128)S(1)}, f32[16,512]{1,0:T(8,128)S(1)}, u32[]{:S(2)}, u32[]{:S(2)}) collective-permute-start(f32[16,512]{1,0:T(8,128)S(1)} %fusion), channel_id=1, source_target_pairs={{0,57},{1,58},{2,59},{3,60},{4,61},{5,62},{6,63},{7,64},{8,65},{9,... | collective-permute-start | bytes 98312
  1203.9 29.6 %collective-permute-start.57 = (f32[16,512]{1,0:T(8,128)S(1)}, f32[16,512]{1,0:T(8,128)S(1)}, u32[]{:S(2)}, u32[]{:S(2)}) collective-permute-start(f32[16,512]{1,0:T(8,128)S(1)} %fusion), channel_id=1, source_target_pairs={{0,58},{1,59},{2,60},{3,61},{4,62},{5,63},{6,64},{7,65},{8,66},{9,... | collective-permute-start | bytes 98312
  1205.9 29.6 %collective-permute-start.58 = (f32[16,512]{1,0:T(8,128)S(1)}, f32[16,512]{1,0:T(8,128)S(1)}, u32[]{:S(2)}, u32[]{:S(2)}) collective-permute-start(f32[16,512]{1,0:T(8,128)S(1)} %fusion), channel_id=1, source_target_pairs={{0,59},{1,60},{2,61},{3,62},{4,63},{5,64},{6,65},{7,66},{8,67},{9,... | collective-permute-start | bytes 98312
  1207.8 29.6 %collective-permute-start.59 = (f32[16,512]{1,0:T(8,128)S(1)}, f32[16,512]{1,0:T(8,128)S(1)}, u32[]{:S(2)}, u32[]{:S(2)}) collective-permute-start(f32[16,512]{1,0:T(8,128)S(1)} %fusion), channel_id=1, source_target_pairs={{0,60},{1,61},{2,62},{3,63},{4,64},{5,65},{6,66},{7,67},{8,68},{9,... | collective-permute-start | bytes 98312
  1209.8 40.4 %collective-permute-start.6 = (f32[16,512]{1,0:T(8,128)S(1)}, f32[16,512]{1,0:T(8,128)S(1)}, u32[]{:S(2)}, u32[]{:S(2)}) collective-permute-start(f32[16,512]{1,0:T(8,128)S(1)} %fusion), channel_id=1, source_target_pairs={{0,7},{1,8},{2,9},{3,10},{4,11},{5,12},{6,13},{7,14},{8,15},{9,16}... | collective-permute-start | bytes 98312
  1227.1 36.2 %collective-permute-start.60 = (f32[16,512]{1,0:T(8,128)S(1)}, f32[16,512]{1,0:T(8,128)S(1)}, u32[]{:S(2)}, u32[]{:S(2)}) collective-permute-start(f32[16,512]{1,0:T(8,128)S(1)} %fusion), channel_id=1, source_target_pairs={{0,61},{1,62},{2,63},{3,64},{4,65},{5,66},{6,67},{7,68},{8,69},{9,... | collective-permute-start | bytes 98312
  1233.6 43.2 %collective-permute-start.61 = (f32[16,512]{1,0:T(8,128)S(1)}, f32[16,512]{1,0:T(8,128)S(1)}, u32[]{:S(2)}, u32[]{:S(2)}) collective-permute-start(f32[16,512]{1,0:T(8,128)S(1)} %fusion), channel_id=1, source_target_pairs={{0,62},{1,63},{2,64},{3,65},{4,66},{5,67},{6,68},{7,69},{8,70},{9,... | collective-permute-start | bytes 98312
  1235.6 41.3 %collective-permute-start.62 = (f32[16,512]{1,0:T(8,128)S(1)}, f32[16,512]{1,0:T(8,128)S(1)}, u32[]{:S(2)}, u32[]{:S(2)}) collective-permute-start(f32[16,512]{1,0:T(8,128)S(1)} %fusion), channel_id=1, source_target_pairs={{0,63},{1,64},{2,65},{3,66},{4,67},{5,68},{6,69},{7,70},{8,71},{9,... | collective-permute-start | bytes 98312
  1237.5 39.3 %collective-permute-start.7 = (f32[16,512]{1,0:T(8,128)S(1)}, f32[16,512]{1,0:T(8,128)S(1)}, u32[]{:S(2)}, u32[]{:S(2)}) collective-permute-start(f32[16,512]{1,0:T(8,128)S(1)} %fusion), channel_id=1, source_target_pairs={{0,8},{1,9},{2,10},{3,11},{4,12},{5,13},{6,14},{7,15},{8,16},{9,17... | collective-permute-start | bytes 98312
  1250.2 26.7 %collective-permute-start.8 = (f32[16,512]{1,0:T(8,128)S(1)}, f32[16,512]{1,0:T(8,128)S(1)}, u32[]{:S(2)}, u32[]{:S(2)}) collective-permute-start(f32[16,512]{1,0:T(8,128)S(1)} %fusion), channel_id=1, source_target_pairs={{0,9},{1,10},{2,11},{3,12},{4,13},{5,14},{6,15},{7,16},{8,17},{9,1... | collective-permute-start | bytes 98312
  1263.3 21.7 %collective-permute-start.9 = (f32[16,512]{1,0:T(8,128)S(1)}, f32[16,512]{1,0:T(8,128)}, u32[]{:S(2)}, u32[]{:S(2)}) collective-permute-start(f32[16,512]{1,0:T(8,128)S(1)} %fusion), channel_id=1, source_target_pairs={{0,10},{1,11},{2,12},{3,13},{4,14},{5,15},{6,16},{7,17},{8,18},{9,... | collective-permute-start | bytes 98312
  (29 other events, 1708.5 us)
